TPU v7x, 32 devices: a whole 2x2x4 slice. The times are simulated.
32 devices in a mesh: shot: 4 (over x, core), band: 4 (over z), net: 2 (over y).
Axes of the slice: x: 2, y: 2, z: 4, core: 2. Of those that a mesh axis runs over, the one named last changes fastest.
Arguments:
- velocity: float32 [128, 1024], P('band'), may hold values from 1.5 to 4
- wave_now: float32 [16, 128, 1024], P(('shot', 'net'), 'band'), may hold values from -6 to 6
- wave_before: float32 [16, 128, 1024], P(('shot', 'net'), 'band'), may hold values from -6 to 6
- adjoint_last: float32 [16, 128, 1024], P(('shot', 'net'), 'band'), may hold values from -6 to 6
- adjoint_after: float32 [16, 128, 1024], P(('shot', 'net'), 'band'), may hold values from -6 to 6
- wavelet: float32 [16, 16], P(('shot', 'net')), may hold values from -72 to 72
- source_col: int32 [16], P(('shot', 'net')), may hold values from 0 to 1023
- rec_first: int32 [16], P(('shot', 'net')), may hold values from 0 to 1022
- rec_last: int32 [16], P(('shot', 'net')), may hold values from 1 to 1023
- rec_count: int32 [16], P(('shot', 'net')), may hold values from 2 to 128, as said below
- observed: float32 [16, 16, 128], P(('shot', 'net')), may hold values from -72 to 72
- conv_in: float32 [32, 18], replicated, may hold values from -1.5 to 1.5
- conv_mid: float32 [32, 288], replicated, may hold values from -0.375 to 0.375
- conv_out: float32 [1, 288], replicated, may hold values from -0.375 to 0.375
- cotangent: float32 [128, 1024], P('band', ('shot', 'net')), may hold values from -0.06629126 to 0.06629126
Outputs:
- new_velocity: float32 [128, 1024], P('band', ('shot', 'net'))
- grad_in: float32 [32, 18], replicated
- grad_mid: float32 [32, 288], replicated
- grad_out: float32 [1, 288], replicated
Inputs may be any that keep to these rules, and one draw needn't show every extreme that they name: rec_last - rec_first >= rec_count - 1 for every shot; some shot has 128 receivers.
All inputs are finite; a program needn't handle non-finite values.
Results may differ from a plain program's by a relative error of at most 0.0003.
Values sent between devices are 32-bit elements; how exact they have to be, the bound alone decides.
A program may use at most 128 MiB of HBM per device.

v0:
```python
import jax
import jax.numpy as jnp
from jax import lax
from jax.sharding import PartitionSpec as P

coefficients = (-205.0 / 72.0, 8.0 / 5.0, -1.0 / 5.0, 8.0 / 315.0, -1.0 / 560.0)
speed_factor = 0.11
source_depth = 2
receiver_depth = 3
highest = lax.Precision.HIGHEST


def extended_2(block, sides, width):
    for axis, dim in sides:
        count = lax.axis_size(axis)
        forward = [(i, i + 1) for i in range(count - 1)]
        backward = [(target, source) for source, target in forward]
        low = lax.ppermute(
            lax.slice_in_dim(block, block.shape[dim] - width, None, axis=dim), axis, forward
        )
        high = lax.ppermute(lax.slice_in_dim(block, 0, width, axis=dim), axis, backward)
        block = jnp.concatenate([low, block, high], axis=dim)
    return block


def laplace(extended):
    middle = extended[..., 4:-4, :]
    height = middle.shape[-2]
    breadth = middle.shape[-1]
    padding = [(0, 0)] * (middle.ndim - 1) + [(4, 4)]
    padded = jnp.pad(middle, padding)
    running = 2.0 * coefficients[0] * middle
    for reach in range(1, 5):
        vertical = (
            extended[..., 4 - reach : 4 - reach + height, :]
            + extended[..., 4 + reach : 4 + reach + height, :]
        )
        lateral = (
            padded[..., 4 - reach : 4 - reach + breadth]
            + padded[..., 4 + reach : 4 + reach + breadth]
        )
        running = running + coefficients[reach] * (vertical + lateral)
    return running


def receiver_table(rec_first, rec_last, rec_count, breadth, slots):
    columns = jnp.arange(breadth, dtype=jnp.int32)
    slot_ids = jnp.arange(slots, dtype=jnp.int32)
    placed = (
        rec_first[:, None]
        + slot_ids[None, :] * (rec_last - rec_first)[:, None] // (rec_count - 1)[:, None]
    )
    active = slot_ids[None, :] < rec_count[:, None]
    return ((columns[None, :, None] == placed[:, None, :]) & active[:, None, :]).astype(jnp.float32)


def patches(extended, height, breadth):
    parts = [
        extended[:, down : down + height, across : across + breadth]
        for down in range(3)
        for across in range(3)
    ]
    return jnp.concatenate(parts, 0).reshape(-1, height * breadth)


def flipped(weights):
    outputs = weights.shape[0]
    channels = weights.shape[1] // 9
    return (
        weights.reshape(outputs, 9, channels)[:, ::-1, :]
        .transpose(2, 1, 0)
        .reshape(channels, 9 * outputs)
    )


def sigmoid_slope(values):
    squashed = jax.nn.sigmoid(values)
    return squashed * (1.0 + values * (1.0 - squashed))


def matmul(left, right):
    return jnp.dot(left, right, precision=highest)


def outer_sum(left, right):
    return lax.dot_general(left, right, (((1,), (1,)), ((), ())), precision=highest)


def on_device(
    velocity,
    wave_now,
    wave_before,
    adjoint_last,
    adjoint_after,
    wavelet,
    source_col,
    rec_first,
    rec_last,
    rec_count,
    observed,
    conv_in,
    conv_mid,
    conv_out,
    cotangent,
):
    rows_here = velocity.shape[0]
    breadth = velocity.shape[1]
    shot_here = wave_now.shape[0]
    num_steps = wavelet.shape[1]
    slots = observed.shape[2]
    piece_cols = cotangent.shape[1]
    first_row = lax.axis_index("band") * rows_here
    speed_sq = (velocity * speed_factor) ** 2
    columns = jnp.arange(breadth, dtype=jnp.int32)
    source_cols = (columns[None, :] == source_col[:, None]).astype(jnp.float32)[:, None, :]
    table = receiver_table(rec_first, rec_last, rec_count, breadth, slots)
    active = (jnp.arange(slots, dtype=jnp.int32)[None, :] < rec_count[:, None]).astype(jnp.float32)

    def source_term(row_start, height, amount):
        row_ids = row_start + jnp.arange(height, dtype=jnp.int32)
        marked = (row_ids == source_depth).astype(jnp.float32)[None, :, None]
        return marked * source_cols * amount[:, None, None]

    def receiver_term(row_start, height, residual):
        row_ids = row_start + jnp.arange(height, dtype=jnp.int32)
        marked = (row_ids == receiver_depth).astype(jnp.float32)[None, :, None]
        injected = jnp.einsum("swk,sk->sw", table, residual, precision=highest)
        return marked * injected[:, None, :]

    speed_wide = extended_2(speed_sq, (("band", 0),), 16)

    def propagate(start, prior, drive, inject):
        grouped = drive.reshape((num_steps // 4, 4) + drive.shape[1:])

        def block(carry, amounts):
            stacked = extended_2(jnp.stack([carry[0], carry[1]]), (("band", 2),), 16)
            current = stacked[0]
            earlier = stacked[1]
            margin = 16
            saved = []
            for offset in range(4):
                inner = margin - 4
                speed_part = speed_wide[16 - inner : 16 + rows_here + inner]
                fresh = (
                    2.0 * current[:, 4:-4]
                    - earlier[:, 4:-4]
                    + speed_part * laplace(current)
                    + inject(first_row - inner, rows_here + 2 * inner, amounts[offset])
                )
                earlier = current[:, 4:-4]
                current = fresh
                margin = inner
                saved.append(fresh[:, inner : inner + rows_here])
            return ((current, earlier), jnp.stack(saved))

        ignored, states = lax.scan(block, (start, prior), grouped)
        return states.reshape((num_steps,) + start.shape)

    stored = propagate(wave_now, wave_before, wavelet.T, source_term)
    samples = jnp.einsum("tsw,swk->tsk", stored[:, :, receiver_depth, :], table, precision=highest)
    misfit = (samples - jnp.transpose(observed, (1, 0, 2))) * active[None]
    adjoint = propagate(adjoint_last, adjoint_after, misfit[::-1], receiver_term)
    imaging = jnp.sum(stored * adjoint[::-1], axis=(0, 1))
    group_count = shot_here * lax.axis_size(("shot", "net"))
    start_col = lax.axis_index(("shot", "net")) * piece_cols
    gathered = lax.psum(imaging, ("shot", "net"))
    summed = lax.dynamic_slice_in_dim(gathered, start_col, piece_cols, 1)
    scaled = summed / float(num_steps * group_count) ** 0.5
    velocity_piece = lax.dynamic_slice_in_dim(velocity, start_col, piece_cols, 1)

    def spread(field):
        extended = extended_2(field, (("band", 1), (("shot", "net"), 2)), 1)
        return patches(extended, rows_here, piece_cols)

    layer_zero = spread(jnp.stack([velocity_piece, scaled]))
    before_one = matmul(conv_in, layer_zero)
    hidden_one = jax.nn.silu(before_one)
    layer_one = spread(hidden_one.reshape(-1, rows_here, piece_cols))
    before_two = matmul(conv_mid, layer_one)
    hidden_two = jax.nn.silu(before_two)
    layer_two = spread(hidden_two.reshape(-1, rows_here, piece_cols))
    update = matmul(conv_out, layer_two).reshape(rows_here, piece_cols)
    new_velocity = velocity_piece + update
    grad_out = outer_sum(cotangent.reshape(1, -1), layer_two)
    slope_two = matmul(flipped(conv_out), spread(cotangent[None])) * sigmoid_slope(before_two)
    grad_mid = outer_sum(slope_two, layer_one)
    slope_one = matmul(
        flipped(conv_mid), spread(slope_two.reshape(-1, rows_here, piece_cols))
    ) * sigmoid_slope(before_one)
    grad_in = outer_sum(slope_one, layer_zero)
    totals = lax.psum((grad_in, grad_mid, grad_out), ("shot", "band", "net"))
    return (new_velocity, totals[0], totals[1], totals[2])


def solution(mesh):
    in_specs = (
        P("band", None),
        P(("shot", "net"), "band", None),
        P(("shot", "net"), "band", None),
        P(("shot", "net"), "band", None),
        P(("shot", "net"), "band", None),
        P(("shot", "net"), None),
        P(("shot", "net")),
        P(("shot", "net")),
        P(("shot", "net")),
        P(("shot", "net")),
        P(("shot", "net"), None, None),
        P(),
        P(),
        P(),
        P("band", ("shot", "net")),
    )
    out_specs = (P("band", ("shot", "net")), P(), P(), P())
    return jax.shard_map(
        on_device, mesh=mesh, in_specs=in_specs, out_specs=out_specs, check_vma=False
    )
```

profile of v0, /device:TPU:0, one launch (start us, length us, event | category | flops | bytes accessed | tf_op | source)
XLA Modules:
  0.0 534.4 jit_solution(12603834938900833449)
XLA Ops:
  8.0 4.9 collective-permute-start.18
  15.2 4.5 collective-permute-start.4
  31.4 4.5 collective-permute-start.20
  40.0 62.5 %while.34 = (s32[]{:T(128)}, f32[2,32,1024]{2,1,0:T(8,128)S(1)}, f32[2,32,1024]{2,1,0:T(8,128)S(1)}, f32[4,4,2,32,1024]{4,3,2,1,0:T(8,128)}, f32[64,1024]{1,0:T(...) while((s32[]{:T(128)}, f32[2,32,1024]{2,1,0:T(8,128)S(1)}, ...), condition=%wide.region_1.2_spmd.clone, body=%wide.region_0.1_spmd.clone.sunk | while | flops 11801106 | bytes 31434516 | solution.py:156
  41.3 5.2 collective-permute-start.1
  46.7 3.9 collective-permute-done
  58.0 5.0 collective-permute-start.1
  73.7 5.0 collective-permute-start.1
  88.8 5.0 collective-permute-start.1
  102.5 4.6 copy.175
  110.2 61.6 %while.35 = (s32[]{:T(128)}, f32[2,32,1024]{2,1,0:T(8,128)S(1)}, f32[2,32,1024]{2,1,0:T(8,128)S(1)}, f32[4,4,2,32,1024]{4,3,2,1,0:T(8,128)}, f32[64,1024]{1,0:T(...) while((s32[]{:T(128)}, f32[2,32,1024]{2,1,0:T(8,128)S(1)}, ...), condition=%wide.region_3.4_spmd.clone, body=%wide.region_2.3_spmd.clone.sunk | while | flops 27165204 | bytes 31534800 | solution.py:156
  112.0 5.0 collective-permute-start.3
  127.6 4.6 collective-permute-start.3
  142.8 4.6 collective-permute-start.3
  158.0 4.6 collective-permute-start.3
  171.8 6.6 %copy.176 = f32[16,2,32,1024]{3,0,1,2:T(8,128)} copy(f32[16,2,32,1024]{3,2,1,0:T(8,128)} %bitcast.368) | data formatting | bytes 8388608 | tf_op jit(solution)/shard_map/reshape | solution.py:157
  178.4 6.8 %rev.13 = f32[16,2,32,1024]{3,0,1,2:T(8,128)} reverse(f32[16,2,32,1024]{3,0,1,2:T(8,128)} %copy.176), dimensions={0} | reverse | bytes 8388608 | tf_op jit(solution)/shard_map/rev | solution.py:163
  185.3 7.0 %multiply_reduce_fusion = f32[32,1024]{1,0:T(8,128)} fusion(f32[16,2,32,1024]{3,0,1,2:T(8,128)} %rev.13, f32[16,2,32,1024]{3,2,1,0:T(8,128)} %bitcast.367), kind=kLoop, calls=%fused_computation.332 | loop fusion | flops 2064384 | bytes 8519680 | tf_op jit(solution)/shard_map/reduce_sum | solution.py:163
  192.4 55.1 %all-reduce.11.cloned.1.call-done = f32[32,1024]{1,0:T(8,128)} async-done(((f32[32,1024]{1,0:T(8,128)}), f32[32,1024]{1,0:T(8,128)}) %all-reduce.11.cloned.1.call-update) | async-done | bytes 131088 | tf_op jit(solution)/shard_map/psum | solution.py:166
  258.5 4.5 collective-permute-start.8
  268.2 5.1 collective-permute-start.10
  285.7 5.3 collective-permute-start.12
  293.0 4.4 pad_maximum_fusion.4
  336.8 4.7 fusion.230
  344.4 5.1 collective-permute-start.14
  357.2 5.1 collective-permute-start.22
  371.7 5.1 collective-permute-start.16
  386.5 5.0 collective-permute-start.24
  411.0 7.1 %pad_maximum_fusion.5 = (f32[32,34,129]{1,0,2:T(8,128)S(1)}, f32[32,34,129]{1,0,2:T(8,128)S(1)}) fusion(f32[32,34,1]{1,0,2:T(8,128)} %collective-permute-done.17, f32[32,1,128]{1,0,2:T(8,128)} %copy.140, f32[32,32,128]{1,0,2:T(8,128)} %copy-done.6, f32[32,1,128]{1,0,2:T(8,128)} %copy.138, f32[32,34,1]{1,0,2:T(8,128)} %collective-permute-done.16), kind=kLoop, calls=%fused_computation.336 | loop fusion | flops 842112 | bytes 1688576 | tf_op jit(solution)/shard_map/concatenate | solution.py:22
  418.1 3.9 fusion.216
  432.5 6.7 %fusion.215 = (f32[32,32,128]{1,0,2:T(8,128)}, f32[32,32,128]{1,0,2:T(8,128)}, f32[32,32,128]{1,0,2:T(8,128)}) fusion(f32[32,34,129]{1,0,2:T(8,128)} %get-tuple-element.522), kind=kLoop, calls=%fused_computation.439 | loop fusion | bytes 3145728 | tf_op jit(solution)/shard_map/slice | solution.py:59
  488.1 39.2 %all-reduce.8 = (f32[32,18]{0,1:T(8,128)}, f32[32,288]{1,0:T(8,128)}, f32[1,288]{1,0:T(1,128)}) all-reduce(f32[32,18]{0,1:T(8,128)S(1)} %copy-done.41, f32[32,288]{1,0:T(8,128)S(1)} %copy-done.38, f32[1,288]{1,0:T(1,128)S(1)} %fusion.231), channel_id=1, replica_groups=mesh['shot'=4,'band'=4,'net'=2] {'shot','band','net'}, use_global_device_ids=true, to_apply=%region_6.7 | all-reduce | flops 10080 | bytes 80640 | tf_op jit(solution)/shard_map/psum | solution.py:191
  (487 shorter events, 278.7 us)
Async XLA Ops:
  7.2 240.3 %all-reduce.11.cloned.1.call-start = ((), (), s32[]{:S(2)}) async-start(), calls=%async_computation | async-start | bytes 262144 | tf_op jit(solution)/shard_map/psum | solution.py:166
  8.0 21.3 %collective-permute-start.18 = (f32[1,1,128]{2,1,0:T(1,128)S(1)}, f32[1,1,128]{2,1,0:T(1,128)S(1)}, u32[]{:S(2)}, u32[]{:S(2)}) collective-permute-start(f32[1,1,128]{2,1,0:T(1,128)S(1)} %get-tuple-element.591), channel_id=1, source_target_pairs={{0,2},{2,4},{4,6},{1,3},{3,5},{5,7},{8,10},{10,12},{12,14},{9,11},... | collective-permute-start | bytes 1544 | tf_op jit(solution)/shard_map/ppermute | solution.py:18
  13.0 16.3 %collective-permute-start.19 = (f32[1,1,128]{2,1,0:T(1,128)S(1)}, f32[1,1,128]{2,1,0:T(1,128)S(1)}, u32[]{:S(2)}, u32[]{:S(2)}) collective-permute-start(f32[1,1,128]{2,1,0:T(1,128)S(1)} %get-tuple-element.592), channel_id=1, source_target_pairs={{2,0},{4,2},{6,4},{3,1},{5,3},{7,5},{10,8},{12,10},{14,12},{11,9},... | collective-permute-start | bytes 1544 | tf_op jit(solution)/shard_map/ppermute | solution.py:21
  15.2 22.1 %collective-permute-start.4 = (f32[16,1024]{1,0:T(8,128)S(1)}, f32[16,1024]{1,0:T(8,128)S(1)}, u32[]{:S(2)}, u32[]{:S(2)}) collective-permute-start(f32[16,1024]{1,0:T(8,128)S(1)} %get-tuple-element.563), channel_id=1, source_target_pairs={{0,2},{2,4},{4,6},{1,3},{3,5},{5,7},{8,10},{10,12},{12,14},{9,11},... | collective-permute-start | bytes 196616 | tf_op jit(solution)/shard_map/ppermute | solution.py:18
  19.8 17.6 %collective-permute-start.5 = (f32[16,1024]{1,0:T(8,128)S(1)}, f32[16,1024]{1,0:T(8,128)S(1)}, u32[]{:S(2)}, u32[]{:S(2)}) collective-permute-start(f32[16,1024]{1,0:T(8,128)S(1)} %get-tuple-element.564), channel_id=1, source_target_pairs={{2,0},{4,2},{6,4},{3,1},{5,3},{7,5},{10,8},{12,10},{14,12},{11,9},... | collective-permute-start | bytes 196616 | tf_op jit(solution)/shard_map/ppermute | solution.py:21
  30.1 162.2 %collective-permute-start.21 = (f32[1,34,1]{2,1,0:T(8,128)S(1)}, f32[1,34,1]{2,1,0:T(8,128)S(1)}, u32[]{:S(2)}, u32[]{:S(2)}) collective-permute-start(f32[1,34,1]{2,1,0:T(8,128)S(1)} %get-tuple-element.585), channel_id=1, source_target_pairs={{1,0},{8,1},{9,8},{16,9},{17,16},{24,17},{25,24},{3,2},{10,3},{11,... | collective-permute-start | bytes 416 | tf_op jit(solution)/shard_map/ppermute | solution.py:21
  31.4 161.0 %collective-permute-start.20 = (f32[1,34,1]{2,1,0:T(8,128)S(1)}, f32[1,34,1]{2,1,0:T(8,128)S(1)}, u32[]{:S(2)}, u32[]{:S(2)}) collective-permute-start(f32[1,34,1]{2,1,0:T(8,128)S(1)} %get-tuple-element.586), channel_id=1, source_target_pairs={{0,1},{1,8},{8,9},{9,16},{16,17},{17,24},{24,25},{2,3},{3,10},{10,... | collective-permute-start | bytes 416 | tf_op jit(solution)/shard_map/ppermute | solution.py:18
  40.0 10.6 %collective-permute-start = (f32[2,2,16,1024]{3,2,1,0:T(8,128)S(1)}, f32[2,2,16,1024]{3,2,1,0:T(8,128)S(1)}, u32[]{:S(2)}, u32[]{:S(2)}) collective-permute-start(f32[2,2,16,1024]{3,2,1,0:T(8,128)S(1)} %get-tuple-element.760), channel_id=1, source_target_pairs={{2,0},{4,2},{6,4},{3,1},{5,3},{7,5},{10,8},{12,10},{14,12},{11,9},... | collective-permute-start | bytes 786440 | tf_op jit(solution)/shard_map/while/body/eval_jaxpr/ppermute | solution.py:21
  41.3 10.5 %collective-permute-start.1 = (f32[2,2,16,1024]{3,2,1,0:T(8,128)S(1)}, f32[2,2,16,1024]{3,2,1,0:T(8,128)S(1)}, u32[]{:S(2)}, u32[]{:S(2)}) collective-permute-start(f32[2,2,16,1024]{3,2,1,0:T(8,128)S(1)} %get-tuple-element.761), channel_id=1, source_target_pairs={{0,2},{2,4},{4,6},{1,3},{3,5},{5,7},{8,10},{10,12},{12,14},{9,11},... | collective-permute-start | bytes 786440 | tf_op jit(solution)/shard_map/while/body/eval_jaxpr/ppermute | solution.py:18
  56.7 9.6 %collective-permute-start = (f32[2,2,16,1024]{3,2,1,0:T(8,128)S(1)}, f32[2,2,16,1024]{3,2,1,0:T(8,128)S(1)}, u32[]{:S(2)}, u32[]{:S(2)}) collective-permute-start(f32[2,2,16,1024]{3,2,1,0:T(8,128)S(1)} %get-tuple-element.760), channel_id=1, source_target_pairs={{2,0},{4,2},{6,4},{3,1},{5,3},{7,5},{10,8},{12,10},{14,12},{11,9},... | collective-permute-start | bytes 786440 | tf_op jit(solution)/shard_map/while/body/eval_jaxpr/ppermute | solution.py:21
  58.0 9.5 %collective-permute-start.1 = (f32[2,2,16,1024]{3,2,1,0:T(8,128)S(1)}, f32[2,2,16,1024]{3,2,1,0:T(8,128)S(1)}, u32[]{:S(2)}, u32[]{:S(2)}) collective-permute-start(f32[2,2,16,1024]{3,2,1,0:T(8,128)S(1)} %get-tuple-element.761), channel_id=1, source_target_pairs={{0,2},{2,4},{4,6},{1,3},{3,5},{5,7},{8,10},{10,12},{12,14},{9,11},... | collective-permute-start | bytes 786440 | tf_op jit(solution)/shard_map/while/body/eval_jaxpr/ppermute | solution.py:18
  72.4 8.8 %collective-permute-start = (f32[2,2,16,1024]{3,2,1,0:T(8,128)S(1)}, f32[2,2,16,1024]{3,2,1,0:T(8,128)S(1)}, u32[]{:S(2)}, u32[]{:S(2)}) collective-permute-start(f32[2,2,16,1024]{3,2,1,0:T(8,128)S(1)} %get-tuple-element.760), channel_id=1, source_target_pairs={{2,0},{4,2},{6,4},{3,1},{5,3},{7,5},{10,8},{12,10},{14,12},{11,9},... | collective-permute-start | bytes 786440 | tf_op jit(solution)/shard_map/while/body/eval_jaxpr/ppermute | solution.py:21
  73.7 8.9 %collective-permute-start.1 = (f32[2,2,16,1024]{3,2,1,0:T(8,128)S(1)}, f32[2,2,16,1024]{3,2,1,0:T(8,128)S(1)}, u32[]{:S(2)}, u32[]{:S(2)}) collective-permute-start(f32[2,2,16,1024]{3,2,1,0:T(8,128)S(1)} %get-tuple-element.761), channel_id=1, source_target_pairs={{0,2},{2,4},{4,6},{1,3},{3,5},{5,7},{8,10},{10,12},{12,14},{9,11},... | collective-permute-start | bytes 786440 | tf_op jit(solution)/shard_map/while/body/eval_jaxpr/ppermute | solution.py:18
  87.5 8.7 %collective-permute-start = (f32[2,2,16,1024]{3,2,1,0:T(8,128)S(1)}, f32[2,2,16,1024]{3,2,1,0:T(8,128)S(1)}, u32[]{:S(2)}, u32[]{:S(2)}) collective-permute-start(f32[2,2,16,1024]{3,2,1,0:T(8,128)S(1)} %get-tuple-element.760), channel_id=1, source_target_pairs={{2,0},{4,2},{6,4},{3,1},{5,3},{7,5},{10,8},{12,10},{14,12},{11,9},... | collective-permute-start | bytes 786440 | tf_op jit(solution)/shard_map/while/body/eval_jaxpr/ppermute | solution.py:21
  88.8 8.9 %collective-permute-start.1 = (f32[2,2,16,1024]{3,2,1,0:T(8,128)S(1)}, f32[2,2,16,1024]{3,2,1,0:T(8,128)S(1)}, u32[]{:S(2)}, u32[]{:S(2)}) collective-permute-start(f32[2,2,16,1024]{3,2,1,0:T(8,128)S(1)} %get-tuple-element.761), channel_id=1, source_target_pairs={{0,2},{2,4},{4,6},{1,3},{3,5},{5,7},{8,10},{10,12},{12,14},{9,11},... | collective-permute-start | bytes 786440 | tf_op jit(solution)/shard_map/while/body/eval_jaxpr/ppermute | solution.py:18
  110.7 10.7 %collective-permute-start.2 = (f32[2,2,16,1024]{3,2,1,0:T(8,128)S(1)}, f32[2,2,16,1024]{3,2,1,0:T(8,128)S(1)}, u32[]{:S(2)}, u32[]{:S(2)}) collective-permute-start(f32[2,2,16,1024]{3,2,1,0:T(8,128)S(1)} %get-tuple-element.783), channel_id=1, source_target_pairs={{2,0},{4,2},{6,4},{3,1},{5,3},{7,5},{10,8},{12,10},{14,12},{11,9},... | collective-permute-start | bytes 786440 | tf_op jit(solution)/shard_map/while/body/eval_jaxpr/ppermute | solution.py:21
  112.0 9.5 %collective-permute-start.3 = (f32[2,2,16,1024]{3,2,1,0:T(8,128)S(1)}, f32[2,2,16,1024]{3,2,1,0:T(8,128)S(1)}, u32[]{:S(2)}, u32[]{:S(2)}) collective-permute-start(f32[2,2,16,1024]{3,2,1,0:T(8,128)S(1)} %get-tuple-element.784), channel_id=1, source_target_pairs={{0,2},{2,4},{4,6},{1,3},{3,5},{5,7},{8,10},{10,12},{12,14},{9,11},... | collective-permute-start | bytes 786440 | tf_op jit(solution)/shard_map/while/body/eval_jaxpr/ppermute | solution.py:18
  126.3 10.3 %collective-permute-start.2 = (f32[2,2,16,1024]{3,2,1,0:T(8,128)S(1)}, f32[2,2,16,1024]{3,2,1,0:T(8,128)S(1)}, u32[]{:S(2)}, u32[]{:S(2)}) collective-permute-start(f32[2,2,16,1024]{3,2,1,0:T(8,128)S(1)} %get-tuple-element.783), channel_id=1, source_target_pairs={{2,0},{4,2},{6,4},{3,1},{5,3},{7,5},{10,8},{12,10},{14,12},{11,9},... | collective-permute-start | bytes 786440 | tf_op jit(solution)/shard_map/while/body/eval_jaxpr/ppermute | solution.py:21
  127.6 9.0 %collective-permute-start.3 = (f32[2,2,16,1024]{3,2,1,0:T(8,128)S(1)}, f32[2,2,16,1024]{3,2,1,0:T(8,128)S(1)}, u32[]{:S(2)}, u32[]{:S(2)}) collective-permute-start(f32[2,2,16,1024]{3,2,1,0:T(8,128)S(1)} %get-tuple-element.784), channel_id=1, source_target_pairs={{0,2},{2,4},{4,6},{1,3},{3,5},{5,7},{8,10},{10,12},{12,14},{9,11},... | collective-permute-start | bytes 786440 | tf_op jit(solution)/shard_map/while/body/eval_jaxpr/ppermute | solution.py:18
  141.5 10.3 %collective-permute-start.2 = (f32[2,2,16,1024]{3,2,1,0:T(8,128)S(1)}, f32[2,2,16,1024]{3,2,1,0:T(8,128)S(1)}, u32[]{:S(2)}, u32[]{:S(2)}) collective-permute-start(f32[2,2,16,1024]{3,2,1,0:T(8,128)S(1)} %get-tuple-element.783), channel_id=1, source_target_pairs={{2,0},{4,2},{6,4},{3,1},{5,3},{7,5},{10,8},{12,10},{14,12},{11,9},... | collective-permute-start | bytes 786440 | tf_op jit(solution)/shard_map/while/body/eval_jaxpr/ppermute | solution.py:21
  142.8 9.0 %collective-permute-start.3 = (f32[2,2,16,1024]{3,2,1,0:T(8,128)S(1)}, f32[2,2,16,1024]{3,2,1,0:T(8,128)S(1)}, u32[]{:S(2)}, u32[]{:S(2)}) collective-permute-start(f32[2,2,16,1024]{3,2,1,0:T(8,128)S(1)} %get-tuple-element.784), channel_id=1, source_target_pairs={{0,2},{2,4},{4,6},{1,3},{3,5},{5,7},{8,10},{10,12},{12,14},{9,11},... | collective-permute-start | bytes 786440 | tf_op jit(solution)/shard_map/while/body/eval_jaxpr/ppermute | solution.py:18
  156.7 10.3 %collective-permute-start.2 = (f32[2,2,16,1024]{3,2,1,0:T(8,128)S(1)}, f32[2,2,16,1024]{3,2,1,0:T(8,128)S(1)}, u32[]{:S(2)}, u32[]{:S(2)}) collective-permute-start(f32[2,2,16,1024]{3,2,1,0:T(8,128)S(1)} %get-tuple-element.783), channel_id=1, source_target_pairs={{2,0},{4,2},{6,4},{3,1},{5,3},{7,5},{10,8},{12,10},{14,12},{11,9},... | collective-permute-start | bytes 786440 | tf_op jit(solution)/shard_map/while/body/eval_jaxpr/ppermute | solution.py:21
  158.0 9.0 %collective-permute-start.3 = (f32[2,2,16,1024]{3,2,1,0:T(8,128)S(1)}, f32[2,2,16,1024]{3,2,1,0:T(8,128)S(1)}, u32[]{:S(2)}, u32[]{:S(2)}) collective-permute-start(f32[2,2,16,1024]{3,2,1,0:T(8,128)S(1)} %get-tuple-element.784), channel_id=1, source_target_pairs={{0,2},{2,4},{4,6},{1,3},{3,5},{5,7},{8,10},{10,12},{12,14},{9,11},... | collective-permute-start | bytes 786440 | tf_op jit(solution)/shard_map/while/body/eval_jaxpr/ppermute | solution.py:18
  266.9 13.5 %collective-permute-start.11 = (f32[32,1,128]{2,0,1:T(8,128)}, f32[32,1,128]{2,0,1:T(8,128)S(1)}, u32[]{:S(2)}, u32[]{:S(2)}) collective-permute-start(f32[32,1,128]{2,0,1:T(8,128)} %bitcast.93), channel_id=1, source_target_pairs={{2,0},{4,2},{6,4},{3,1},{5,3},{7,5},{10,8},{12,10},{14,12},{11,9},... | collective-permute-start | bytes 49160 | tf_op jit(solution)/shard_map/ppermute | solution.py:21
  343.1 22.8 %collective-permute-start.15 = (f32[32,1,128]{2,0,1:T(8,128)}, f32[32,1,128]{2,0,1:T(8,128)S(1)}, u32[]{:S(2)}, u32[]{:S(2)}) collective-permute-start(f32[32,1,128]{2,0,1:T(8,128)} %bitcast.95), channel_id=1, source_target_pairs={{2,0},{4,2},{6,4},{3,1},{5,3},{7,5},{10,8},{12,10},{14,12},{11,9},... | collective-permute-start | bytes 49160 | tf_op jit(solution)/shard_map/ppermute | solution.py:21
  344.4 17.9 %collective-permute-start.14 = (f32[32,1,128]{2,0,1:T(8,128)}, f32[32,1,128]{2,0,1:T(8,128)}, u32[]{:S(2)}, u32[]{:S(2)}) collective-permute-start(f32[32,1,128]{2,0,1:T(8,128)} %bitcast.94), channel_id=1, source_target_pairs={{0,2},{2,4},{4,6},{1,3},{3,5},{5,7},{8,10},{10,12},{12,14},{9,11},... | collective-permute-start | bytes 49160 | tf_op jit(solution)/shard_map/ppermute | solution.py:18
  355.9 24.5 %collective-permute-start.23 = (f32[32,1,128]{2,0,1:T(8,128)}, f32[32,1,128]{2,0,1:T(8,128)}, u32[]{:S(2)}, u32[]{:S(2)}) collective-permute-start(f32[32,1,128]{2,0,1:T(8,128)} %bitcast.436), channel_id=1, source_target_pairs={{2,0},{4,2},{6,4},{3,1},{5,3},{7,5},{10,8},{12,10},{14,12},{11,9},... | collective-permute-start | bytes 49160 | tf_op jit(solution)/shard_map/ppermute | solution.py:21
  357.2 19.7 %collective-permute-start.22 = (f32[32,1,128]{2,0,1:T(8,128)}, f32[32,1,128]{2,0,1:T(8,128)}, u32[]{:S(2)}, u32[]{:S(2)}) collective-permute-start(f32[32,1,128]{2,0,1:T(8,128)} %bitcast.437), channel_id=1, source_target_pairs={{0,2},{2,4},{4,6},{1,3},{3,5},{5,7},{8,10},{10,12},{12,14},{9,11},... | collective-permute-start | bytes 49160 | tf_op jit(solution)/shard_map/ppermute | solution.py:18
  370.3 40.7 %collective-permute-start.17 = (f32[32,34,1]{1,0,2:T(8,128)}, f32[32,34,1]{1,0,2:T(8,128)}, u32[]{:S(2)}, u32[]{:S(2)}) collective-permute-start(f32[32,34,1]{1,0,2:T(8,128)} %get-tuple-element.527), channel_id=1, source_target_pairs={{1,0},{8,1},{9,8},{16,9},{17,16},{24,17},{25,24},{3,2},{10,3},{11,... | collective-permute-start | bytes 13064 | tf_op jit(solution)/shard_map/ppermute | solution.py:21
  371.7 39.3 %collective-permute-start.16 = (f32[32,34,1]{1,0,2:T(8,128)}, f32[32,34,1]{1,0,2:T(8,128)}, u32[]{:S(2)}, u32[]{:S(2)}) collective-permute-start(f32[32,34,1]{1,0,2:T(8,128)} %get-tuple-element.528), channel_id=1, source_target_pairs={{0,1},{1,8},{8,9},{9,16},{16,17},{17,24},{24,25},{2,3},{3,10},{10,... | collective-permute-start | bytes 13064 | tf_op jit(solution)/shard_map/ppermute | solution.py:18
  385.0 10.1 %collective-permute-start.25 = (f32[32,34,1]{1,0,2:T(8,128)S(1)}, f32[32,34,1]{1,0,2:T(8,128)S(1)}, u32[]{:S(2)}, u32[]{:S(2)}) collective-permute-start(f32[32,34,1]{1,0,2:T(8,128)S(1)} %get-tuple-element.523), channel_id=1, source_target_pairs={{1,0},{8,1},{9,8},{16,9},{17,16},{24,17},{25,24},{3,2},{10,3},{11,... | collective-permute-start | bytes 13064 | tf_op jit(solution)/shard_map/ppermute | solution.py:21
  386.5 8.7 %collective-permute-start.24 = (f32[32,34,1]{1,0,2:T(8,128)S(1)}, f32[32,34,1]{1,0,2:T(8,128)S(1)}, u32[]{:S(2)}, u32[]{:S(2)}) collective-permute-start(f32[32,34,1]{1,0,2:T(8,128)S(1)} %get-tuple-element.524), channel_id=1, source_target_pairs={{0,1},{1,8},{8,9},{9,16},{16,17},{17,24},{24,25},{2,3},{3,10},{10,... | collective-permute-start | bytes 13064 | tf_op jit(solution)/shard_map/ppermute | solution.py:18
  (53 other events, 888.7 us)
Sparse Core Ops, SparseCore 0:
  192.4 55.0 all-reduce.10
where the time goes:
time: 544 us; the launch traced here: 534 us
  local copies, waits for them, and re-layouts  169 us (31%)
  starting transfers between devices  117 us (22%)
  other arithmetic  78.2 us (14%)
  waiting for transfers between devices  76.8 us (14%)
  blocking collectives  39.2 us (7%)
  matrix products  37.4 us (7%)
  between operations  15.3 us (3%)
    ppermute x19, starting transfers between devices, extended_2(): lax.ppermute(lax.slice_in_dim(block, block.shape[dim] - width, None, axis...  91.8 us
    slice x25, local copies, waits for them, and re-layouts, patches(): extended[:, down:down + height, across:across + breadth]  83.9 us
    psum x1, waiting for transfers between devices, on_device(): gathered = lax.psum(imaging, ('shot', 'net'))  55.1 us
    psum x1, blocking collectives, on_device(): totals = lax.psum((grad_in, grad_mid, grad_out), ('shot', 'band', 'net'))  39.2 us
    concatenate x23, other arithmetic, extended_2(): block = jnp.concatenate([low, block, high], axis=dim)  27.2 us
    ppermute x19, starting transfers between devices, extended_2(): lax.ppermute(lax.slice_in_dim(block, 0, width, axis=dim), axis, backward)  24.9 us
    unnamed x126, local copies, waits for them, and re-layouts  22.8 us
    add x24, other arithmetic, block(): 2.0 * current[:, 4:-4] - earlier[:, 4:-4] + speed_part * laplace(current)  21.6 us
  transfers between devices with their start and end apart: 39, of which 11 were waited for; matrix products, arithmetic and copies ran while one was open for 28% of the time, Pallas kernels for 0%

commit v1 on v0

--- a/solution.py
+++ b/solution.py
@@ -8,6 +8,12 @@
 source_depth = 2
 receiver_depth = 3
 highest = lax.Precision.HIGHEST
+
+
+def gather_and_add(value, mesh_axis):
+    parts = lax.all_gather(value, mesh_axis, axis=0, tiled=False)
+    acc = parts.sum(axis=0)
+    return acc
 
 
 def extended_2(block, sides, width):
@@ -163,7 +169,7 @@
     imaging = jnp.sum(stored * adjoint[::-1], axis=(0, 1))
     group_count = shot_here * lax.axis_size(("shot", "net"))
     start_col = lax.axis_index(("shot", "net")) * piece_cols
-    gathered = lax.psum(imaging, ("shot", "net"))
+    gathered = gather_and_add(imaging, ("shot", "net"))
     summed = lax.dynamic_slice_in_dim(gathered, start_col, piece_cols, 1)
     scaled = summed / float(num_steps * group_count) ** 0.5
     velocity_piece = lax.dynamic_slice_in_dim(velocity, start_col, piece_cols, 1)

time: 544 us -> 495 us (0.910)
  waiting for transfers between devices: 76.8 us -> 33.6 us
    psum x1 -> x0, waiting for transfers between devices: 55.1 us -> none  [on_device(): gathered = lax.psum(imaging, ('shot', 'net'))]
    all_gather x0 -> x1, waiting for transfers between devices: none -> 9.1 us  [gather_and_add(): parts = lax.all_gather(value, mesh_axis, axis=0, tiled=False)]
  transfers between devices with their start and end apart: 39 -> 39, of which waited for: 11 -> 14; matrix products, arithmetic and copies ran while one was open for 28% -> 16% of each run, Pallas kernels for 0% -> 0%
where the time goes in v1:
time: 495 us; the launch traced here: 486 us
  local copies, waits for them, and re-layouts  167 us (34%)
  starting transfers between devices  115 us (23%)
  other arithmetic  75.4 us (15%)
  blocking collectives  39.3 us (8%)
  matrix products  37.4 us (8%)
  waiting for transfers between devices  33.6 us (7%)
  between operations  15.3 us (3%)
    ppermute x19, starting transfers between devices, extended_2(): lax.ppermute(lax.slice_in_dim(block, block.shape[dim] - width, None, axis...  90.5 us
    slice x25, local copies, waits for them, and re-layouts, patches(): extended[:, down:down + height, across:across + breadth]  83.9 us
    psum x1, blocking collectives, on_device(): totals = lax.psum((grad_in, grad_mid, grad_out), ('shot', 'band', 'net'))  39.3 us
    concatenate x23, other arithmetic, extended_2(): block = jnp.concatenate([low, block, high], axis=dim)  25.1 us
    ppermute x19, starting transfers between devices, extended_2(): lax.ppermute(lax.slice_in_dim(block, 0, width, axis=dim), axis, backward)  24.9 us
    unnamed x126, local copies, waits for them, and re-layouts  22 us
    add x24, other arithmetic, block(): 2.0 * current[:, 4:-4] - earlier[:, 4:-4] + speed_part * laplace(current)  21.6 us
    dot_general x16, matrix products, receiver_term(): injected = jnp.einsum('swk,sk->sw', table, residual, precision=highest)  16.8 us
  transfers between devices with their start and end apart: 39, of which 14 were waited for; matrix products, arithmetic and copies ran while one was open for 16% of the time, Pallas kernels for 0%

profile of v1, /device:TPU:0, one launch (start us, length us, event | category | flops | bytes accessed | tf_op | source)
XLA Modules:
  0.0 485.8 jit_solution(230208720382711872)
XLA Ops:
  8.2 5.0 %collective-permute-start.4 = (f32[16,1024]{1,0:T(8,128)S(1)}, f32[16,1024]{1,0:T(8,128)S(1)}, u32[]{:S(2)}, u32[]{:S(2)}) collective-permute-start(f32[16,1024]{1,0:T(8,128)S(1)} %get-tuple-element.563), channel_id=1, source_target_pairs={{0,2},{2,4},{4,6},{1,3},{3,5},{5,7},{8,10},{10,12},{12,14},{9,11},... | collective-permute-start | bytes 196616 | tf_op jit(solution)/shard_map/ppermute | solution.py:24
  22.0 60.4 %while.34 = (s32[]{:T(128)}, f32[2,32,1024]{2,1,0:T(8,128)S(1)}, f32[2,32,1024]{2,1,0:T(8,128)S(1)}, f32[4,4,2,32,1024]{4,3,2,1,0:T(8,128)}, f32[64,1024]{1,0:T(...) while((s32[]{:T(128)}, f32[2,32,1024]{2,1,0:T(8,128)S(1)}, ...), condition=%wide.region_1.2_spmd.clone, body=%wide.region_0.1_spmd.clone.sunk | while | flops 11801106 | bytes 31434516 | solution.py:162
  23.4 4.6 collective-permute-start.1
  38.5 5.0 %collective-permute-start.1 = (f32[2,2,16,1024]{3,2,1,0:T(8,128)S(1)}, f32[2,2,16,1024]{3,2,1,0:T(8,128)S(1)}, u32[]{:S(2)}, u32[]{:S(2)}) collective-permute-start(f32[2,2,16,1024]{3,2,1,0:T(8,128)S(1)} %get-tuple-element.761), channel_id=1, source_target_pairs={{0,2},{2,4},{4,6},{1,3},{3,5},{5,7},{8,10},{10,12},{12,14},{9,11},... | collective-permute-start | bytes 786440 | tf_op jit(solution)/shard_map/while/body/eval_jaxpr/ppermute | solution.py:24
  53.6 5.0 %collective-permute-start.1 = (f32[2,2,16,1024]{3,2,1,0:T(8,128)S(1)}, f32[2,2,16,1024]{3,2,1,0:T(8,128)S(1)}, u32[]{:S(2)}, u32[]{:S(2)}) collective-permute-start(f32[2,2,16,1024]{3,2,1,0:T(8,128)S(1)} %get-tuple-element.761), channel_id=1, source_target_pairs={{0,2},{2,4},{4,6},{1,3},{3,5},{5,7},{8,10},{10,12},{12,14},{9,11},... | collective-permute-start | bytes 786440 | tf_op jit(solution)/shard_map/while/body/eval_jaxpr/ppermute | solution.py:24
  68.7 5.0 %collective-permute-start.1 = (f32[2,2,16,1024]{3,2,1,0:T(8,128)S(1)}, f32[2,2,16,1024]{3,2,1,0:T(8,128)S(1)}, u32[]{:S(2)}, u32[]{:S(2)}) collective-permute-start(f32[2,2,16,1024]{3,2,1,0:T(8,128)S(1)} %get-tuple-element.761), channel_id=1, source_target_pairs={{0,2},{2,4},{4,6},{1,3},{3,5},{5,7},{8,10},{10,12},{12,14},{9,11},... | collective-permute-start | bytes 786440 | tf_op jit(solution)/shard_map/while/body/eval_jaxpr/ppermute | solution.py:24
  82.4 4.6 copy.175
  90.1 61.6 %while.35 = (s32[]{:T(128)}, f32[2,32,1024]{2,1,0:T(8,128)S(1)}, f32[2,32,1024]{2,1,0:T(8,128)S(1)}, f32[4,4,2,32,1024]{4,3,2,1,0:T(8,128)}, f32[64,1024]{1,0:T(...) while((s32[]{:T(128)}, f32[2,32,1024]{2,1,0:T(8,128)S(1)}, ...), condition=%wide.region_3.4_spmd.clone, body=%wide.region_2.3_spmd.clone.sunk | while | flops 27165204 | bytes 31534800 | solution.py:162
  91.9 5.0 %collective-permute-start.3 = (f32[2,2,16,1024]{3,2,1,0:T(8,128)S(1)}, f32[2,2,16,1024]{3,2,1,0:T(8,128)S(1)}, u32[]{:S(2)}, u32[]{:S(2)}) collective-permute-start(f32[2,2,16,1024]{3,2,1,0:T(8,128)S(1)} %get-tuple-element.784), channel_id=1, source_target_pairs={{0,2},{2,4},{4,6},{1,3},{3,5},{5,7},{8,10},{10,12},{12,14},{9,11},... | collective-permute-start | bytes 786440 | tf_op jit(solution)/shard_map/while/body/eval_jaxpr/ppermute | solution.py:24
  107.5 4.6 collective-permute-start.3
  122.7 4.6 collective-permute-start.3
  137.9 4.6 collective-permute-start.3
  151.7 6.6 %copy.176 = f32[16,2,32,1024]{3,0,1,2:T(8,128)} copy(f32[16,2,32,1024]{3,2,1,0:T(8,128)} %bitcast.369) | data formatting | bytes 8388608 | tf_op jit(solution)/shard_map/reshape | solution.py:163
  158.3 6.8 %rev.13 = f32[16,2,32,1024]{3,0,1,2:T(8,128)} reverse(f32[16,2,32,1024]{3,0,1,2:T(8,128)} %copy.176), dimensions={0} | reverse | bytes 8388608 | tf_op jit(solution)/shard_map/rev | solution.py:169
  165.2 7.0 %multiply_reduce_fusion = f32[32,1024]{1,0:T(8,128)} fusion(f32[16,2,32,1024]{3,0,1,2:T(8,128)} %rev.13, f32[16,2,32,1024]{3,2,1,0:T(8,128)} %bitcast.368), kind=kLoop, calls=%fused_computation.332 | loop fusion | flops 2064384 | bytes 8519680 | tf_op jit(solution)/shard_map/reduce_sum | solution.py:169
  172.3 3.9 collective-permute-start.18
  183.0 4.5 collective-permute-start.20
  189.1 9.1 %all-gather.3.cloned.1.call-done = f32[256,1024]{1,0:T(8,128)} async-done(((f32[32,1024]{1,0:T(8,128)}), f32[256,1024]{1,0:T(8,128)}) %all-gather.3.cloned.1.call-update) | async-done | bytes 1048592 | tf_op jit(solution)/shard_map/all_gather | solution.py:14
  204.3 4.1 collective-permute-done.7
  209.8 4.5 collective-permute-start.8
  219.5 5.1 %collective-permute-start.10 = (f32[32,1,128]{2,0,1:T(8,128)}, f32[32,1,128]{2,0,1:T(8,128)}, u32[]{:S(2)}, u32[]{:S(2)}) collective-permute-start(f32[32,1,128]{2,0,1:T(8,128)} %bitcast.93), channel_id=1, source_target_pairs={{0,2},{2,4},{4,6},{1,3},{3,5},{5,7},{8,10},{10,12},{12,14},{9,11},... | collective-permute-start | bytes 49160 | tf_op jit(solution)/shard_map/ppermute | solution.py:24
  237.0 5.3 %collective-permute-start.12 = (f32[32,34,1]{1,0,2:T(8,128)S(1)}, f32[32,34,1]{1,0,2:T(8,128)S(1)}, u32[]{:S(2)}, u32[]{:S(2)}) collective-permute-start(f32[32,34,1]{1,0,2:T(8,128)S(1)} %get-tuple-element.532), channel_id=1, source_target_pairs={{0,1},{1,8},{8,9},{9,16},{16,17},{17,24},{24,25},{2,3},{3,10},{10,... | collective-permute-start | bytes 13064 | tf_op jit(solution)/shard_map/ppermute | solution.py:24
  244.3 4.4 pad_maximum_fusion.4
  288.1 4.7 fusion.230
  295.7 5.1 %collective-permute-start.14 = (f32[32,1,128]{2,0,1:T(8,128)}, f32[32,1,128]{2,0,1:T(8,128)}, u32[]{:S(2)}, u32[]{:S(2)}) collective-permute-start(f32[32,1,128]{2,0,1:T(8,128)} %bitcast.95), channel_id=1, source_target_pairs={{0,2},{2,4},{4,6},{1,3},{3,5},{5,7},{8,10},{10,12},{12,14},{9,11},... | collective-permute-start | bytes 49160 | tf_op jit(solution)/shard_map/ppermute | solution.py:24
  308.4 5.1 %collective-permute-start.22 = (f32[32,1,128]{2,0,1:T(8,128)}, f32[32,1,128]{2,0,1:T(8,128)}, u32[]{:S(2)}, u32[]{:S(2)}) collective-permute-start(f32[32,1,128]{2,0,1:T(8,128)} %bitcast.439), channel_id=1, source_target_pairs={{0,2},{2,4},{4,6},{1,3},{3,5},{5,7},{8,10},{10,12},{12,14},{9,11},... | collective-permute-start | bytes 49160 | tf_op jit(solution)/shard_map/ppermute | solution.py:24
  323.0 5.1 %collective-permute-start.16 = (f32[32,34,1]{1,0,2:T(8,128)}, f32[32,34,1]{1,0,2:T(8,128)}, u32[]{:S(2)}, u32[]{:S(2)}) collective-permute-start(f32[32,34,1]{1,0,2:T(8,128)} %get-tuple-element.528), channel_id=1, source_target_pairs={{0,1},{1,8},{8,9},{9,16},{16,17},{17,24},{24,25},{2,3},{3,10},{10,... | collective-permute-start | bytes 13064 | tf_op jit(solution)/shard_map/ppermute | solution.py:24
  337.7 5.0 %collective-permute-start.24 = (f32[32,34,1]{1,0,2:T(8,128)S(1)}, f32[32,34,1]{1,0,2:T(8,128)S(1)}, u32[]{:S(2)}, u32[]{:S(2)}) collective-permute-start(f32[32,34,1]{1,0,2:T(8,128)S(1)} %get-tuple-element.524), channel_id=1, source_target_pairs={{0,1},{1,8},{8,9},{9,16},{16,17},{17,24},{24,25},{2,3},{3,10},{10,... | collective-permute-start | bytes 13064 | tf_op jit(solution)/shard_map/ppermute | solution.py:24
  362.2 7.1 %pad_maximum_fusion.5 = (f32[32,34,129]{1,0,2:T(8,128)S(1)}, f32[32,34,129]{1,0,2:T(8,128)S(1)}) fusion(f32[32,34,1]{1,0,2:T(8,128)} %collective-permute-done.17, f32[32,1,128]{1,0,2:T(8,128)} %copy.140, f32[32,32,128]{1,0,2:T(8,128)} %copy-done.6, f32[32,1,128]{1,0,2:T(8,128)} %copy.138, f32[32,34,1]{1,0,2:T(8,128)} %collective-permute-done.16), kind=kLoop, calls=%fused_computation.336 | loop fusion | flops 842112 | bytes 1688576 | tf_op jit(solution)/shard_map/concatenate | solution.py:28
  369.4 3.9 fusion.216
  383.8 6.7 %fusion.215 = (f32[32,32,128]{1,0,2:T(8,128)}, f32[32,32,128]{1,0,2:T(8,128)}, f32[32,32,128]{1,0,2:T(8,128)}) fusion(f32[32,34,129]{1,0,2:T(8,128)} %get-tuple-element.522), kind=kLoop, calls=%fused_computation.439 | loop fusion | bytes 3145728 | tf_op jit(solution)/shard_map/slice | solution.py:65
  439.4 39.3 %all-reduce.8 = (f32[32,18]{0,1:T(8,128)}, f32[32,288]{1,0:T(8,128)}, f32[1,288]{1,0:T(1,128)}) all-reduce(f32[32,18]{0,1:T(8,128)S(1)} %copy-done.40, f32[32,288]{1,0:T(8,128)S(1)} %copy-done.39, f32[1,288]{1,0:T(1,128)S(1)} %fusion.231), channel_id=1, replica_groups=mesh['shot'=4,'band'=4,'net'=2] {'shot','band','net'}, use_global_device_ids=true, to_apply=%region_6.7 | all-reduce | flops 10080 | bytes 80640 | tf_op jit(solution)/shard_map/psum | solution.py:197
  (488 shorter events, 276.9 us)
Async XLA Ops:
  7.2 191.0 %all-gather.3.cloned.1.call-start = ((), (), s32[]{:S(2)}) async-start(), calls=%async_computation | async-start | bytes 1179648 | tf_op jit(solution)/shard_map/all_gather | solution.py:14
  8.2 9.9 %collective-permute-start.4 = (f32[16,1024]{1,0:T(8,128)S(1)}, f32[16,1024]{1,0:T(8,128)S(1)}, u32[]{:S(2)}, u32[]{:S(2)}) collective-permute-start(f32[16,1024]{1,0:T(8,128)S(1)} %get-tuple-element.563), channel_id=1, source_target_pairs={{0,2},{2,4},{4,6},{1,3},{3,5},{5,7},{8,10},{10,12},{12,14},{9,11},... | collective-permute-start | bytes 196616 | tf_op jit(solution)/shard_map/ppermute | solution.py:24
  22.1 9.1 %collective-permute-start = (f32[2,2,16,1024]{3,2,1,0:T(8,128)S(1)}, f32[2,2,16,1024]{3,2,1,0:T(8,128)S(1)}, u32[]{:S(2)}, u32[]{:S(2)}) collective-permute-start(f32[2,2,16,1024]{3,2,1,0:T(8,128)S(1)} %get-tuple-element.760), channel_id=1, source_target_pairs={{2,0},{4,2},{6,4},{3,1},{5,3},{7,5},{10,8},{12,10},{14,12},{11,9},... | collective-permute-start | bytes 786440 | tf_op jit(solution)/shard_map/while/body/eval_jaxpr/ppermute | solution.py:27
  23.4 9.0 %collective-permute-start.1 = (f32[2,2,16,1024]{3,2,1,0:T(8,128)S(1)}, f32[2,2,16,1024]{3,2,1,0:T(8,128)S(1)}, u32[]{:S(2)}, u32[]{:S(2)}) collective-permute-start(f32[2,2,16,1024]{3,2,1,0:T(8,128)S(1)} %get-tuple-element.761), channel_id=1, source_target_pairs={{0,2},{2,4},{4,6},{1,3},{3,5},{5,7},{8,10},{10,12},{12,14},{9,11},... | collective-permute-start | bytes 786440 | tf_op jit(solution)/shard_map/while/body/eval_jaxpr/ppermute | solution.py:24
  37.2 8.7 %collective-permute-start = (f32[2,2,16,1024]{3,2,1,0:T(8,128)S(1)}, f32[2,2,16,1024]{3,2,1,0:T(8,128)S(1)}, u32[]{:S(2)}, u32[]{:S(2)}) collective-permute-start(f32[2,2,16,1024]{3,2,1,0:T(8,128)S(1)} %get-tuple-element.760), channel_id=1, source_target_pairs={{2,0},{4,2},{6,4},{3,1},{5,3},{7,5},{10,8},{12,10},{14,12},{11,9},... | collective-permute-start | bytes 786440 | tf_op jit(solution)/shard_map/while/body/eval_jaxpr/ppermute | solution.py:27
  38.5 8.9 %collective-permute-start.1 = (f32[2,2,16,1024]{3,2,1,0:T(8,128)S(1)}, f32[2,2,16,1024]{3,2,1,0:T(8,128)S(1)}, u32[]{:S(2)}, u32[]{:S(2)}) collective-permute-start(f32[2,2,16,1024]{3,2,1,0:T(8,128)S(1)} %get-tuple-element.761), channel_id=1, source_target_pairs={{0,2},{2,4},{4,6},{1,3},{3,5},{5,7},{8,10},{10,12},{12,14},{9,11},... | collective-permute-start | bytes 786440 | tf_op jit(solution)/shard_map/while/body/eval_jaxpr/ppermute | solution.py:24
  52.3 8.7 %collective-permute-start = (f32[2,2,16,1024]{3,2,1,0:T(8,128)S(1)}, f32[2,2,16,1024]{3,2,1,0:T(8,128)S(1)}, u32[]{:S(2)}, u32[]{:S(2)}) collective-permute-start(f32[2,2,16,1024]{3,2,1,0:T(8,128)S(1)} %get-tuple-element.760), channel_id=1, source_target_pairs={{2,0},{4,2},{6,4},{3,1},{5,3},{7,5},{10,8},{12,10},{14,12},{11,9},... | collective-permute-start | bytes 786440 | tf_op jit(solution)/shard_map/while/body/eval_jaxpr/ppermute | solution.py:27
  53.6 8.9 %collective-permute-start.1 = (f32[2,2,16,1024]{3,2,1,0:T(8,128)S(1)}, f32[2,2,16,1024]{3,2,1,0:T(8,128)S(1)}, u32[]{:S(2)}, u32[]{:S(2)}) collective-permute-start(f32[2,2,16,1024]{3,2,1,0:T(8,128)S(1)} %get-tuple-element.761), channel_id=1, source_target_pairs={{0,2},{2,4},{4,6},{1,3},{3,5},{5,7},{8,10},{10,12},{12,14},{9,11},... | collective-permute-start | bytes 786440 | tf_op jit(solution)/shard_map/while/body/eval_jaxpr/ppermute | solution.py:24
  67.4 8.7 %collective-permute-start = (f32[2,2,16,1024]{3,2,1,0:T(8,128)S(1)}, f32[2,2,16,1024]{3,2,1,0:T(8,128)S(1)}, u32[]{:S(2)}, u32[]{:S(2)}) collective-permute-start(f32[2,2,16,1024]{3,2,1,0:T(8,128)S(1)} %get-tuple-element.760), channel_id=1, source_target_pairs={{2,0},{4,2},{6,4},{3,1},{5,3},{7,5},{10,8},{12,10},{14,12},{11,9},... | collective-permute-start | bytes 786440 | tf_op jit(solution)/shard_map/while/body/eval_jaxpr/ppermute | solution.py:27
  68.7 8.9 %collective-permute-start.1 = (f32[2,2,16,1024]{3,2,1,0:T(8,128)S(1)}, f32[2,2,16,1024]{3,2,1,0:T(8,128)S(1)}, u32[]{:S(2)}, u32[]{:S(2)}) collective-permute-start(f32[2,2,16,1024]{3,2,1,0:T(8,128)S(1)} %get-tuple-element.761), channel_id=1, source_target_pairs={{0,2},{2,4},{4,6},{1,3},{3,5},{5,7},{8,10},{10,12},{12,14},{9,11},... | collective-permute-start | bytes 786440 | tf_op jit(solution)/shard_map/while/body/eval_jaxpr/ppermute | solution.py:24
  90.6 10.7 %collective-permute-start.2 = (f32[2,2,16,1024]{3,2,1,0:T(8,128)S(1)}, f32[2,2,16,1024]{3,2,1,0:T(8,128)S(1)}, u32[]{:S(2)}, u32[]{:S(2)}) collective-permute-start(f32[2,2,16,1024]{3,2,1,0:T(8,128)S(1)} %get-tuple-element.783), channel_id=1, source_target_pairs={{2,0},{4,2},{6,4},{3,1},{5,3},{7,5},{10,8},{12,10},{14,12},{11,9},... | collective-permute-start | bytes 786440 | tf_op jit(solution)/shard_map/while/body/eval_jaxpr/ppermute | solution.py:27
  91.9 9.5 %collective-permute-start.3 = (f32[2,2,16,1024]{3,2,1,0:T(8,128)S(1)}, f32[2,2,16,1024]{3,2,1,0:T(8,128)S(1)}, u32[]{:S(2)}, u32[]{:S(2)}) collective-permute-start(f32[2,2,16,1024]{3,2,1,0:T(8,128)S(1)} %get-tuple-element.784), channel_id=1, source_target_pairs={{0,2},{2,4},{4,6},{1,3},{3,5},{5,7},{8,10},{10,12},{12,14},{9,11},... | collective-permute-start | bytes 786440 | tf_op jit(solution)/shard_map/while/body/eval_jaxpr/ppermute | solution.py:24
  106.2 10.3 %collective-permute-start.2 = (f32[2,2,16,1024]{3,2,1,0:T(8,128)S(1)}, f32[2,2,16,1024]{3,2,1,0:T(8,128)S(1)}, u32[]{:S(2)}, u32[]{:S(2)}) collective-permute-start(f32[2,2,16,1024]{3,2,1,0:T(8,128)S(1)} %get-tuple-element.783), channel_id=1, source_target_pairs={{2,0},{4,2},{6,4},{3,1},{5,3},{7,5},{10,8},{12,10},{14,12},{11,9},... | collective-permute-start | bytes 786440 | tf_op jit(solution)/shard_map/while/body/eval_jaxpr/ppermute | solution.py:27
  107.5 9.0 %collective-permute-start.3 = (f32[2,2,16,1024]{3,2,1,0:T(8,128)S(1)}, f32[2,2,16,1024]{3,2,1,0:T(8,128)S(1)}, u32[]{:S(2)}, u32[]{:S(2)}) collective-permute-start(f32[2,2,16,1024]{3,2,1,0:T(8,128)S(1)} %get-tuple-element.784), channel_id=1, source_target_pairs={{0,2},{2,4},{4,6},{1,3},{3,5},{5,7},{8,10},{10,12},{12,14},{9,11},... | collective-permute-start | bytes 786440 | tf_op jit(solution)/shard_map/while/body/eval_jaxpr/ppermute | solution.py:24
  121.4 10.3 %collective-permute-start.2 = (f32[2,2,16,1024]{3,2,1,0:T(8,128)S(1)}, f32[2,2,16,1024]{3,2,1,0:T(8,128)S(1)}, u32[]{:S(2)}, u32[]{:S(2)}) collective-permute-start(f32[2,2,16,1024]{3,2,1,0:T(8,128)S(1)} %get-tuple-element.783), channel_id=1, source_target_pairs={{2,0},{4,2},{6,4},{3,1},{5,3},{7,5},{10,8},{12,10},{14,12},{11,9},... | collective-permute-start | bytes 786440 | tf_op jit(solution)/shard_map/while/body/eval_jaxpr/ppermute | solution.py:27
  122.7 9.0 %collective-permute-start.3 = (f32[2,2,16,1024]{3,2,1,0:T(8,128)S(1)}, f32[2,2,16,1024]{3,2,1,0:T(8,128)S(1)}, u32[]{:S(2)}, u32[]{:S(2)}) collective-permute-start(f32[2,2,16,1024]{3,2,1,0:T(8,128)S(1)} %get-tuple-element.784), channel_id=1, source_target_pairs={{0,2},{2,4},{4,6},{1,3},{3,5},{5,7},{8,10},{10,12},{12,14},{9,11},... | collective-permute-start | bytes 786440 | tf_op jit(solution)/shard_map/while/body/eval_jaxpr/ppermute | solution.py:24
  136.6 10.3 %collective-permute-start.2 = (f32[2,2,16,1024]{3,2,1,0:T(8,128)S(1)}, f32[2,2,16,1024]{3,2,1,0:T(8,128)S(1)}, u32[]{:S(2)}, u32[]{:S(2)}) collective-permute-start(f32[2,2,16,1024]{3,2,1,0:T(8,128)S(1)} %get-tuple-element.783), channel_id=1, source_target_pairs={{2,0},{4,2},{6,4},{3,1},{5,3},{7,5},{10,8},{12,10},{14,12},{11,9},... | collective-permute-start | bytes 786440 | tf_op jit(solution)/shard_map/while/body/eval_jaxpr/ppermute | solution.py:27
  137.9 9.0 %collective-permute-start.3 = (f32[2,2,16,1024]{3,2,1,0:T(8,128)S(1)}, f32[2,2,16,1024]{3,2,1,0:T(8,128)S(1)}, u32[]{:S(2)}, u32[]{:S(2)}) collective-permute-start(f32[2,2,16,1024]{3,2,1,0:T(8,128)S(1)} %get-tuple-element.784), channel_id=1, source_target_pairs={{0,2},{2,4},{4,6},{1,3},{3,5},{5,7},{8,10},{10,12},{12,14},{9,11},... | collective-permute-start | bytes 786440 | tf_op jit(solution)/shard_map/while/body/eval_jaxpr/ppermute | solution.py:24
  172.3 8.3 %collective-permute-start.18 = (f32[1,1,128]{2,1,0:T(1,128)S(1)}, f32[1,1,128]{2,1,0:T(1,128)S(1)}, u32[]{:S(2)}, u32[]{:S(2)}) collective-permute-start(f32[1,1,128]{2,1,0:T(1,128)S(1)} %get-tuple-element.591), channel_id=1, source_target_pairs={{0,2},{2,4},{4,6},{1,3},{3,5},{5,7},{8,10},{10,12},{12,14},{9,11},... | collective-permute-start | bytes 1544 | tf_op jit(solution)/shard_map/ppermute | solution.py:24
  209.8 6.2 %collective-permute-start.8 = (f32[2,34,1]{2,1,0:T(8,128)S(1)}, f32[2,34,1]{2,1,0:T(8,128)S(1)}, u32[]{:S(2)}, u32[]{:S(2)}) collective-permute-start(f32[2,34,1]{2,1,0:T(8,128)S(1)} %get-tuple-element.578), channel_id=1, source_target_pairs={{0,1},{1,8},{8,9},{9,16},{16,17},{17,24},{24,25},{2,3},{3,10},{10,... | collective-permute-start | bytes 824 | tf_op jit(solution)/shard_map/ppermute | solution.py:24
  218.2 13.5 %collective-permute-start.11 = (f32[32,1,128]{2,0,1:T(8,128)}, f32[32,1,128]{2,0,1:T(8,128)S(1)}, u32[]{:S(2)}, u32[]{:S(2)}) collective-permute-start(f32[32,1,128]{2,0,1:T(8,128)} %bitcast.94), channel_id=1, source_target_pairs={{2,0},{4,2},{6,4},{3,1},{5,3},{7,5},{10,8},{12,10},{14,12},{11,9},... | collective-permute-start | bytes 49160 | tf_op jit(solution)/shard_map/ppermute | solution.py:27
  219.5 8.6 %collective-permute-start.10 = (f32[32,1,128]{2,0,1:T(8,128)}, f32[32,1,128]{2,0,1:T(8,128)}, u32[]{:S(2)}, u32[]{:S(2)}) collective-permute-start(f32[32,1,128]{2,0,1:T(8,128)} %bitcast.93), channel_id=1, source_target_pairs={{0,2},{2,4},{4,6},{1,3},{3,5},{5,7},{8,10},{10,12},{12,14},{9,11},... | collective-permute-start | bytes 49160 | tf_op jit(solution)/shard_map/ppermute | solution.py:24
  235.6 8.7 %collective-permute-start.13 = (f32[32,34,1]{1,0,2:T(8,128)S(1)}, f32[32,34,1]{1,0,2:T(8,128)S(1)}, u32[]{:S(2)}, u32[]{:S(2)}) collective-permute-start(f32[32,34,1]{1,0,2:T(8,128)S(1)} %get-tuple-element.531), channel_id=1, source_target_pairs={{1,0},{8,1},{9,8},{16,9},{17,16},{24,17},{25,24},{3,2},{10,3},{11,... | collective-permute-start | bytes 13064 | tf_op jit(solution)/shard_map/ppermute | solution.py:27
  237.0 7.2 %collective-permute-start.12 = (f32[32,34,1]{1,0,2:T(8,128)S(1)}, f32[32,34,1]{1,0,2:T(8,128)S(1)}, u32[]{:S(2)}, u32[]{:S(2)}) collective-permute-start(f32[32,34,1]{1,0,2:T(8,128)S(1)} %get-tuple-element.532), channel_id=1, source_target_pairs={{0,1},{1,8},{8,9},{9,16},{16,17},{17,24},{24,25},{2,3},{3,10},{10,... | collective-permute-start | bytes 13064 | tf_op jit(solution)/shard_map/ppermute | solution.py:24
  294.4 22.8 %collective-permute-start.15 = (f32[32,1,128]{2,0,1:T(8,128)}, f32[32,1,128]{2,0,1:T(8,128)S(1)}, u32[]{:S(2)}, u32[]{:S(2)}) collective-permute-start(f32[32,1,128]{2,0,1:T(8,128)} %bitcast.96), channel_id=1, source_target_pairs={{2,0},{4,2},{6,4},{3,1},{5,3},{7,5},{10,8},{12,10},{14,12},{11,9},... | collective-permute-start | bytes 49160 | tf_op jit(solution)/shard_map/ppermute | solution.py:27
  295.7 17.9 %collective-permute-start.14 = (f32[32,1,128]{2,0,1:T(8,128)}, f32[32,1,128]{2,0,1:T(8,128)}, u32[]{:S(2)}, u32[]{:S(2)}) collective-permute-start(f32[32,1,128]{2,0,1:T(8,128)} %bitcast.95), channel_id=1, source_target_pairs={{0,2},{2,4},{4,6},{1,3},{3,5},{5,7},{8,10},{10,12},{12,14},{9,11},... | collective-permute-start | bytes 49160 | tf_op jit(solution)/shard_map/ppermute | solution.py:24
  307.1 24.5 %collective-permute-start.23 = (f32[32,1,128]{2,0,1:T(8,128)}, f32[32,1,128]{2,0,1:T(8,128)}, u32[]{:S(2)}, u32[]{:S(2)}) collective-permute-start(f32[32,1,128]{2,0,1:T(8,128)} %bitcast.438), channel_id=1, source_target_pairs={{2,0},{4,2},{6,4},{3,1},{5,3},{7,5},{10,8},{12,10},{14,12},{11,9},... | collective-permute-start | bytes 49160 | tf_op jit(solution)/shard_map/ppermute | solution.py:27
  308.4 19.7 %collective-permute-start.22 = (f32[32,1,128]{2,0,1:T(8,128)}, f32[32,1,128]{2,0,1:T(8,128)}, u32[]{:S(2)}, u32[]{:S(2)}) collective-permute-start(f32[32,1,128]{2,0,1:T(8,128)} %bitcast.439), channel_id=1, source_target_pairs={{0,2},{2,4},{4,6},{1,3},{3,5},{5,7},{8,10},{10,12},{12,14},{9,11},... | collective-permute-start | bytes 49160 | tf_op jit(solution)/shard_map/ppermute | solution.py:24
  321.5 40.7 %collective-permute-start.17 = (f32[32,34,1]{1,0,2:T(8,128)}, f32[32,34,1]{1,0,2:T(8,128)}, u32[]{:S(2)}, u32[]{:S(2)}) collective-permute-start(f32[32,34,1]{1,0,2:T(8,128)} %get-tuple-element.527), channel_id=1, source_target_pairs={{1,0},{8,1},{9,8},{16,9},{17,16},{24,17},{25,24},{3,2},{10,3},{11,... | collective-permute-start | bytes 13064 | tf_op jit(solution)/shard_map/ppermute | solution.py:27
  323.0 39.3 %collective-permute-start.16 = (f32[32,34,1]{1,0,2:T(8,128)}, f32[32,34,1]{1,0,2:T(8,128)}, u32[]{:S(2)}, u32[]{:S(2)}) collective-permute-start(f32[32,34,1]{1,0,2:T(8,128)} %get-tuple-element.528), channel_id=1, source_target_pairs={{0,1},{1,8},{8,9},{9,16},{16,17},{17,24},{24,25},{2,3},{3,10},{10,... | collective-permute-start | bytes 13064 | tf_op jit(solution)/shard_map/ppermute | solution.py:24
  336.3 10.1 %collective-permute-start.25 = (f32[32,34,1]{1,0,2:T(8,128)S(1)}, f32[32,34,1]{1,0,2:T(8,128)S(1)}, u32[]{:S(2)}, u32[]{:S(2)}) collective-permute-start(f32[32,34,1]{1,0,2:T(8,128)S(1)} %get-tuple-element.523), channel_id=1, source_target_pairs={{1,0},{8,1},{9,8},{16,9},{17,16},{24,17},{25,24},{3,2},{10,3},{11,... | collective-permute-start | bytes 13064 | tf_op jit(solution)/shard_map/ppermute | solution.py:27
  337.7 8.7 %collective-permute-start.24 = (f32[32,34,1]{1,0,2:T(8,128)S(1)}, f32[32,34,1]{1,0,2:T(8,128)S(1)}, u32[]{:S(2)}, u32[]{:S(2)}) collective-permute-start(f32[32,34,1]{1,0,2:T(8,128)S(1)} %get-tuple-element.524), channel_id=1, source_target_pairs={{0,1},{1,8},{8,9},{9,16},{16,17},{17,24},{24,25},{2,3},{3,10},{10,... | collective-permute-start | bytes 13064 | tf_op jit(solution)/shard_map/ppermute | solution.py:24
  (53 other events, 642.2 us)
Sparse Core Ops, SparseCore 0:
  172.4 25.8 all-gather.2
